TPU v7x, 32 devices: a whole 2x2x4 slice. The times are simulated.
32 devices in a mesh: groups: 2 (over x), tm: 16 (over z, y, core).
Axes of the slice: x: 2, y: 2, z: 4, core: 2. Of those that a mesh axis runs over, the one named last changes fastest.
Arguments:
- initial_value: float32 [1024, 1024], P('groups'), parts along dimension 0, may hold values from -3 to 3
- guess: float32 [32, 512, 1024], P(('groups', 'tm')), parts along dimension 0, may hold values from -3 to 3
- rate_field: float32 [512, 1024], replicated, may hold values from 0.1 to 1
- strength: float32 [2], P('groups'), parts along dimension 0, may hold values from 0.2 to 0.8
Outputs:
- solution: float32 [32, 512, 1024], P(('groups', 'tm')), parts along dimension 0
There are 2 independent parts, one for each index of `groups`. A program takes and returns all parts, laid end to end along the dimension named above; an argument that names none is the same for every part. Nothing has to cross between parts.
All inputs are finite; a program needn't handle non-finite values.
Results may differ from a plain program's by a relative error of at most 0.0003.
Values sent between devices are 32-bit elements; how exact they have to be, the bound alone decides.
No kernel may reach another device: no remote copies, remote signals or barrier semaphores. Data moves between devices by JAX's collectives and lax.ppermute only.
A program may use at most 64 MiB of HBM per device.

v0:
```python
import math

import jax
import jax.numpy as jnp
from jax import lax
from jax.sharding import PartitionSpec as P

SWEEPS = 2


alpha_factor = 0.05
diffusion = 1.0
linear_part = 0.5
highest = lax.Precision.HIGHEST


def shifted(value, axis, steps):
    count = lax.axis_size(axis)
    leading, last = (max(0, -steps), min(count, count - steps))
    return lax.ppermute(value, axis, [(source, source + steps) for source in range(leading, last)])


def sine_table(order_n):
    ramp = jnp.arange(order_n, dtype=jnp.int32) + 1
    folded = ramp[:, None] * ramp[None, :] % (2 * (order_n + 1))
    return math.sqrt(2.0 / (order_n + 1)) * jnp.sin(
        jnp.pi * folded.astype(jnp.float32) / (order_n + 1)
    )


def sine_eigen(ramp_rows, order_n):
    angle = jnp.pi * (ramp_rows.astype(jnp.float32) + 1.0) / (2.0 * (order_n + 1))
    sines = jnp.sin(angle)
    return 4.0 * sines * sines


def time_tables(step_count):
    ramp = jnp.arange(step_count, dtype=jnp.int32)
    folded = ramp[:, None] * ramp[None, :] % step_count
    angle = 2.0 * jnp.pi * folded.astype(jnp.float32) / step_count
    return (jnp.cos(angle), jnp.sin(angle))


def laplace(surface):
    padded = jnp.pad(surface, 1)
    return (
        padded[2:, 1:-1] + padded[:-2, 1:-1] + padded[1:-1, 2:] + padded[1:-1, :-2] - 4.0 * surface
    )


def operator(surface, rate_field, strength_value):
    return (
        surface
        - diffusion * laplace(surface)
        + strength_value * rate_field * surface * (1.0 + surface * surface)
    )


def to_sine(surface, row_table, col_table):
    return jnp.dot(jnp.dot(row_table, surface, precision=highest), col_table, precision=highest)


def modal_solve(flat, cos_t, sin_t, real_den, imag_den, step_count):
    part_re = jnp.dot(cos_t, flat, precision=highest)
    part_im = -jnp.dot(sin_t, flat, precision=highest)
    magnitude = real_den * real_den + imag_den * imag_den
    sol_re = -(part_re * real_den + part_im * imag_den) / magnitude
    sol_im = -(part_im * real_den - part_re * imag_den) / magnitude
    return (
        jnp.dot(cos_t, sol_re, precision=highest) - jnp.dot(sin_t, sol_im, precision=highest)
    ) / step_count


def body(initial_value, guess, rate_field, strength):
    step_count = lax.axis_size("tm")
    position = lax.axis_index("tm")
    state = guess[0]
    total_rows, total_cols = state.shape
    row_block = total_rows // step_count
    row_table = sine_table(total_rows)
    col_table = sine_table(total_cols)
    strength_value = strength[0]
    log_ratio = math.log(alpha_factor) / step_count
    ratio_g = math.exp(log_ratio)
    own_scale = jnp.exp(position.astype(jnp.float32) * log_ratio)
    cos_t, sin_t = time_tables(step_count)
    first_row = position * row_block
    my_rows = first_row + jnp.arange(row_block, dtype=jnp.int32)
    eigen_sum = (
        sine_eigen(my_rows, total_rows)[:, None]
        + sine_eigen(jnp.arange(total_cols, dtype=jnp.int32), total_cols)[None, :]
    ).reshape(-1)
    real_den = (1.0 + linear_part * strength_value - ratio_g * cos_t[:, 1])[
        :, None
    ] + diffusion * eigen_sum[None, :]
    imag_den = (ratio_g * sin_t[:, 1])[:, None]
    for sweep_index in range(SWEEPS):
        earlier = shifted(state, "tm", 1)
        earlier = jnp.where(position == 0, initial_value, earlier)
        spectral = to_sine(
            operator(state, rate_field, strength_value) - earlier, row_table, col_table
        )
        gathered = lax.all_to_all(
            (spectral * own_scale)[None], "tm", split_axis=1, concat_axis=0, tiled=True
        )
        flat = gathered.reshape(step_count, -1)
        solved = modal_solve(flat, cos_t, sin_t, real_den, imag_den, step_count).reshape(
            gathered.shape
        )
        returned = lax.all_to_all(solved, "tm", split_axis=0, concat_axis=1, tiled=True)
        state = state + to_sine(returned[0] / own_scale, row_table, col_table)
    return state[None]


def solution(mesh):
    in_specs = (P("groups", None), P(("groups", "tm"), None, None), P(), P("groups"))
    out_specs = P(("groups", "tm"), None, None)
    return jax.shard_map(body, mesh=mesh, in_specs=in_specs, out_specs=out_specs, check_vma=False)
```

profile of v0, /device:TPU:1, one launch (start us, length us, event | category | flops | bytes accessed | tf_op | source)
XLA Modules:
  0.0 446.1 jit_solution(12542223351881929041)
XLA Ops:
  0.0 4.5 %collective-permute-start = (f32[512,1024]{1,0:T(8,128)}, f32[512,1024]{1,0:T(8,128)S(1)}, u32[]{:S(2)}, u32[]{:S(2)}) collective-permute-start(f32[512,1024]{1,0:T(8,128)} %bitcast.47), channel_id=1, source_target_pairs={{0,1},{1,2},{2,3},{3,4},{4,5},{5,6},{6,7},{7,8},{8,9},{9,10},{10,1... | collective-permute-start | bytes 6291464 | tf_op jit(solution)/shard_map/ppermute | solution.py:20
  5.2 22.6 %collective-permute-done = f32[512,1024]{1,0:T(8,128)S(1)} collective-permute-done((f32[512,1024]{1,0:T(8,128)}, f32[512,1024]{1,0:T(8,128)S(1)}, u32[]{:S(2)}, u32[]{:S(2)}) %collective-permute-start) | collective-permute-done | bytes 2097184 | tf_op jit(solution)/shard_map/ppermute | solution.py:20
  27.8 14.4 %fusion.16 = f32[512,1024]{1,0:T(8,128)S(1)} fusion(f32[512,1024]{1,0:T(8,128)} %bitcast.48, f32[512,1024]{1,0:T(8,128)} %param.4, f32[512,1024]{1,0:T(8,128)S(1)} %collective-permute-done, f32[512,1024]{1,0:T(8,128)} %param.6, f32[]{:T(128)} %bitcast.34, pred[]{:T(512)S(6)} %eq.10, s32[512]{0:T(512)S(1)} %iota_add_fusion.1), kind=kOutput, calls=%fused_computation.35 | convolution fusion | flops 3231186944 | bytes 10489861 | tf_op jit(solution)/shard_map/dot_general | solution.py:60
  42.2 24.0 %multiply_bitcast_fusion.1 = f32[1,512,1024]{2,1,0:T(8,128)S(1)} fusion(f32[512,1024]{1,0:T(8,128)S(1)} %fusion.16, s32[1024]{0:T(1024)S(1)} %iota_add_fusion, f32[]{:T(128)S(6)} %exp.3), kind=kOutput, calls=%fused_computation.67 | convolution fusion | flops 6453460992 | bytes 4198404 | tf_op jit(solution)/shard_map/dot_general | solution.py:60
  66.2 3.5 copy.5
  69.7 7.1 %all-to-all-start = ((f32[1,512,1024]{2,0,1:T(1,128)}), f32[1,512,1024]{2,0,1:T(1,128)S(1)}, u32[]{:S(2)}, u32[]{:S(2)}) async-start(f32[1,512,1024]{2,0,1:T(1,128)} %copy.5), calls=%async_computation | async-start | bytes 4194304 | tf_op jit(solution)/shard_map/all_to_all | solution.py:103
  77.2 41.2 %all-to-all-done = f32[1,512,1024]{2,0,1:T(1,128)S(1)} async-done(((f32[1,512,1024]{2,0,1:T(1,128)}), f32[1,512,1024]{2,0,1:T(1,128)S(1)}, u32[]{:S(2)}, u32[]{:S(2)}) %all-to-all-start) | async-done | bytes 2097184 | tf_op jit(solution)/shard_map/all_to_all | solution.py:103
  118.3 6.8 %reduce = f32[512,1024]{1,0:T(8,128)} reduce(f32[1,512,1024]{2,0,1:T(1,128)S(1)} %all-to-all-done, f32[]{:T(128)} %constant.103), dimensions={0}, to_apply=%all_to_all.8.reduce_sub_computation | reduce | bytes 4194308 | tf_op jit(solution)/shard_map/all_to_all | solution.py:103
  131.1 2.4 fusion.68
  133.5 2.5 fusion.1
  137.2 58.4 %all_to_all.16 = f32[16,32,1024]{2,1,0:T(8,128)S(1)} all-to-all(f32[16,32,1024]{2,1,0:T(8,128)S(1)} %bitcast.37), channel_id=1, replica_groups=mesh['groups'=2,'tm'=16] {'tm'}, dimensions={0} | all-to-all | bytes 4194304 | tf_op jit(solution)/shard_map/all_to_all | solution.py:110
  195.8 7.5 %fusion.115 = f32[512,1024]{1,0:T(8,128)S(1)} fusion(f32[512,1024]{1,0:T(8,128)S(1)} %bitcast.42, s32[512]{0:T(512)S(1)} %iota_add_fusion.1), kind=kOutput, calls=%fused_computation.119 | convolution fusion | flops 3223846912 | bytes 4196352 | tf_op jit(solution)/shard_map/dot_general | solution.py:60
  203.4 23.8 %fusion.74 = f32[512,1024]{1,0:T(8,128)S(1)} fusion(f32[512,1024]{1,0:T(8,128)S(1)} %fusion.115, s32[1024]{0:T(1024)S(1)} %iota_add_fusion, f32[1,512,1024]{2,1,0:T(8,128)S(1)} %copy-done), kind=kOutput, calls=%fused_computation.83 | convolution fusion | flops 6453460992 | bytes 6295552 | tf_op jit(solution)/shard_map/dot_general | solution.py:60
  227.2 2.5 collective-permute-start.1
  229.8 22.8 %collective-permute-done.1 = f32[512,1024]{1,0:T(8,128)S(1)} collective-permute-done((f32[512,1024]{1,0:T(8,128)S(1)}, f32[512,1024]{1,0:T(8,128)S(1)}, u32[]{:S(2)}, u32[]{:S(2)}) %collective-permute-start.1) | collective-permute-done | bytes 2097184 | tf_op jit(solution)/shard_map/ppermute | solution.py:20
  252.6 9.1 %fusion.25 = f32[512,1024]{1,0:T(8,128)S(1)} fusion(f32[512,1024]{1,0:T(8,128)S(1)} %fusion.74, f32[512,1024]{1,0:T(8,128)S(1)} %copy-done.1, f32[512,1024]{1,0:T(8,128)S(1)} %collective-permute-done.1, f32[512,1024]{1,0:T(8,128)S(1)} %copy-done.2, f32[]{:T(128)} %bitcast.36, pred[]{:T(512)S(6)} %eq.10, s32[512]{0:T(512)S(1)} %iota_add_fusion.1), kind=kOutput, calls=%fused_computation.43 | convolution fusion | flops 3231186944 | bytes 10489861 | tf_op jit(solution)/shard_map/dot_general | solution.py:60
  261.7 24.0 %multiply_bitcast_fusion = f32[1,512,1024]{2,1,0:T(8,128)S(1)} fusion(f32[512,1024]{1,0:T(8,128)S(1)} %fusion.25, s32[1024]{0:T(1024)S(1)} %iota_add_fusion, f32[]{:T(128)S(6)} %exp.3), kind=kOutput, calls=%fused_computation.59 | convolution fusion | flops 6453460992 | bytes 4198404 | tf_op jit(solution)/shard_map/dot_general | solution.py:60
  287.8 54.5 %all_to_all.17 = f32[1,512,1024]{2,0,1:T(1,128)S(1)} all-to-all(f32[1,512,1024]{2,0,1:T(1,128)S(1)} %copy.6), channel_id=1, replica_groups=mesh['groups'=2,'tm'=16] {'tm'}, dimensions={1} | all-to-all | bytes 4194304 | tf_op jit(solution)/shard_map/all_to_all | solution.py:103
  342.3 6.8 %reduce.1 = f32[512,1024]{1,0:T(8,128)} reduce(f32[1,512,1024]{2,0,1:T(1,128)S(1)} %all_to_all.17, f32[]{:T(128)} %constant.103), dimensions={0}, to_apply=%all_to_all.10.reduce_sub_computation | reduce | bytes 4194308 | tf_op jit(solution)/shard_map/all_to_all | solution.py:103
  355.1 2.4 fusion.66
  357.5 2.5 fusion
  361.2 52.3 %all_to_all.18 = f32[16,32,1024]{2,1,0:T(8,128)S(1)} all-to-all(f32[16,32,1024]{2,1,0:T(8,128)S(1)} %bitcast.38), channel_id=1, replica_groups=mesh['groups'=2,'tm'=16] {'tm'}, dimensions={0} | all-to-all | bytes 4194304 | tf_op jit(solution)/shard_map/all_to_all | solution.py:110
  413.8 7.5 %fusion.112 = f32[512,1024]{1,0:T(8,128)S(1)} fusion(f32[512,1024]{1,0:T(8,128)S(1)} %bitcast.41, s32[512]{0:T(512)S(1)} %iota_add_fusion.1), kind=kOutput, calls=%fused_computation.118 | convolution fusion | flops 3223846912 | bytes 4196352 | tf_op jit(solution)/shard_map/dot_general | solution.py:60
  421.3 24.4 %add_bitcast_fusion = f32[1,512,1024]{2,1,0:T(8,128)} fusion(f32[512,1024]{1,0:T(8,128)S(1)} %copy-done.4, f32[512,1024]{1,0:T(8,128)S(1)} %fusion.112, s32[1024]{0:T(1024)S(1)} %iota_add_fusion), kind=kOutput, calls=%fused_computation.57 | convolution fusion | flops 6453460992 | bytes 6295552 | tf_op jit(solution)/shard_map/dot_general | solution.py:60
  (30 shorter events, 17.3 us)
Async XLA Ops:
  0.0 27.8 %collective-permute-start = (f32[512,1024]{1,0:T(8,128)}, f32[512,1024]{1,0:T(8,128)S(1)}, u32[]{:S(2)}, u32[]{:S(2)}) collective-permute-start(f32[512,1024]{1,0:T(8,128)} %bitcast.47), channel_id=1, source_target_pairs={{0,1},{1,2},{2,3},{3,4},{4,5},{5,6},{6,7},{7,8},{8,9},{9,10},{10,1... | collective-permute-start | bytes 6291464 | tf_op jit(solution)/shard_map/ppermute | solution.py:20
  69.7 48.6 %all-to-all-start = ((f32[1,512,1024]{2,0,1:T(1,128)}), f32[1,512,1024]{2,0,1:T(1,128)S(1)}, u32[]{:S(2)}, u32[]{:S(2)}) async-start(f32[1,512,1024]{2,0,1:T(1,128)} %copy.5), calls=%async_computation | async-start | bytes 4194304 | tf_op jit(solution)/shard_map/all_to_all | solution.py:103
  195.8 7.5 %copy-start = (f32[1,512,1024]{2,1,0:T(8,128)S(1)}, f32[1,512,1024]{2,1,0:T(8,128)}, u32[]{:S(2)}) copy-start(f32[1,512,1024]{2,1,0:T(8,128)} %param.5) | copy-start | bytes 6291460
  203.4 49.2 %copy-start.1 = (f32[512,1024]{1,0:T(8,128)S(1)}, f32[512,1024]{1,0:T(8,128)}, u32[]{:S(2)}) copy-start(f32[512,1024]{1,0:T(8,128)} %param.4) | copy-start | bytes 6291460
  203.4 49.2 %copy-start.2 = (f32[512,1024]{1,0:T(8,128)S(1)}, f32[512,1024]{1,0:T(8,128)}, u32[]{:S(2)}) copy-start(f32[512,1024]{1,0:T(8,128)} %param.6) | copy-start | bytes 6291460
  227.2 25.3 %copy-start.3 = (f32[512,1024]{1,0:T(8,128)}, f32[512,1024]{1,0:T(8,128)S(1)}, u32[]{:S(2)}) copy-start(f32[512,1024]{1,0:T(8,128)S(1)} %fusion.74) | copy-start | bytes 6291460
  227.2 25.3 %collective-permute-start.1 = (f32[512,1024]{1,0:T(8,128)S(1)}, f32[512,1024]{1,0:T(8,128)S(1)}, u32[]{:S(2)}, u32[]{:S(2)}) collective-permute-start(f32[512,1024]{1,0:T(8,128)S(1)} %fusion.74), channel_id=1, source_target_pairs={{0,1},{1,2},{2,3},{3,4},{4,5},{5,6},{6,7},{7,8},{8,9},{9,10},{10,1... | collective-permute-start | bytes 6291464 | tf_op jit(solution)/shard_map/ppermute | solution.py:20
  413.8 7.5 %copy-start.4 = (f32[512,1024]{1,0:T(8,128)S(1)}, f32[512,1024]{1,0:T(8,128)}, u32[]{:S(2)}) copy-start(f32[512,1024]{1,0:T(8,128)} %copy-done.3) | copy-start | bytes 6291460
where the time goes:
time: 453 us; the launch traced here: 446 us
  blocking collectives  165 us (36%)
  matrix products  152 us (34%)
  waiting for transfers between devices  86.5 us (19%)
  other arithmetic  14.5 us (3%)
  starting transfers between devices  14.1 us (3%)
  local copies, waits for them, and re-layouts  12 us (3%)
    all_to_all x2, blocking collectives, body(): lax.all_to_all(solved, 'tm', split_axis=0, concat_axis=1, tiled=True)  111 us
    dot_general x4, matrix products, to_sine(): jnp.dot(jnp.dot(row_table, surface, precision=highest), col_table, precis...  96.1 us
    all_to_all x1, blocking collectives, body(): lax.all_to_all((spectral * own_scale)[None], 'tm', split_axis=1, concat_a...  54.5 us
    ppermute x2, waiting for transfers between devices, shifted(): lax.ppermute(value, axis, [(source, source + steps) for source in range(l...  45.3 us
    all_to_all x1, waiting for transfers between devices, body(): lax.all_to_all((spectral * own_scale)[None], 'tm', split_axis=1, concat_a...  41.2 us
    dot_general x4, matrix products, to_sine(): jnp.dot(row_table, surface, precision=highest)  38.6 us
    all_to_all x2, other arithmetic, body(): lax.all_to_all((spectral * own_scale)[None], 'tm', split_axis=1, concat_a...  13.7 us
  transfers between devices with their start and end apart: 3, of which 3 were waited for; matrix products, arithmetic and copies ran while one was open for 0% of the time, Pallas kernels for 0%

commit v1 on v0

v1 whole, which is shorter than its diff:
```python
import math

import jax
import jax.numpy as jnp
import numpy as np
from jax import lax
from jax.experimental import pallas as pl
from jax.experimental.pallas import tpu as pltpu
from jax.sharding import PartitionSpec as P

SWEEPS = 2

alpha_factor = 0.05
diffusion = 1.0
linear_part = 0.5
f32 = jnp.float32
bf16 = jnp.bfloat16
VMEM = pl.BlockSpec(memory_space=pltpu.VMEM)
SMEM = pl.BlockSpec(memory_space=pltpu.SMEM)


def halves(matrix):
    high = matrix.astype(bf16)
    low = (matrix - high.astype(np.float64)).astype(bf16)
    return high, low


def sine_halves(order):
    ramp = np.arange(order, dtype=np.int64) + 1
    folded = ramp[:, None] * ramp[None, :] % (2 * (order + 1))
    full = math.sqrt(2.0 / (order + 1)) * np.sin(np.pi * folded / (order + 1))
    half = order // 2
    return np.stack([full[0::2, :half], full[1::2, :half]])


def sine_eigen(order):
    ramp = np.arange(order, dtype=np.float64)
    value = 4.0 * np.sin(np.pi * (ramp + 1.0) / (2.0 * (order + 1))) ** 2
    return np.concatenate([value[0::2], value[1::2]]).astype(np.float32)


def reversal(size):
    return np.eye(size)[::-1].astype(bf16)


def split(value):
    high = value.astype(bf16)
    return high, (value - high.astype(f32)).astype(bf16)


def product(left, right, dims):
    return lax.dot_general(left, right, ((dims), ((), ())), preferred_element_type=f32)


def apply_right(value, high, low, transposed):
    dims = ((1,), (0,)) if transposed else ((1,), (1,))
    top, rest = split(value)
    return product(top, high, dims) + (product(top, low, dims) + product(rest, high, dims))


def apply_left(high, low, value):
    dims = ((1,), (0,))
    top, rest = split(value)
    return product(high, top, dims) + (product(low, top, dims) + product(high, rest, dims))


def flip_rows(value, mirror):
    size = mirror.shape[0]
    count = value.shape[0] // size
    pieces = []
    for index in range(count):
        block = value[(count - 1 - index) * size : (count - index) * size]
        top, rest = split(block)
        dims = ((1,), (0,))
        pieces.append(product(mirror, top, dims) + product(mirror, rest, dims))
    return pieces[0] if count == 1 else jnp.concatenate(pieces, axis=0)


def flip_cols(value, mirror):
    size = mirror.shape[0]
    count = value.shape[1] // size
    pieces = []
    for index in range(count):
        block = value[:, (count - 1 - index) * size : (count - index) * size]
        top, rest = split(block)
        dims = ((1,), (0,))
        pieces.append(product(top, mirror, dims) + product(rest, mirror, dims))
    return pieces[0] if count == 1 else jnp.concatenate(pieces, axis=1)


def react(state, rate, strength):
    return strength * state * (linear_part - rate * (1.0 + state * state))


def to_modes(get, tables, write):
    sxh, sxl, syh, syl = tables
    for col in range(2):
        for row in range(2):
            sign_r = 1.0 if row == 0 else -1.0
            sign_c = 1.0 if col == 0 else -1.0
            left = get(0, 0) + sign_r * get(1, 0)
            right = get(0, 1) + sign_r * get(1, 1)
            part = left + sign_c * right
            part = apply_right(part, syh[col], syl[col], False)
            write(row, col, apply_left(sxh[row], sxl[row], part))


def from_modes(get, tables):
    txh, txl, syh, syl = tables
    part = [[None, None], [None, None]]
    for col in range(2):
        for row in range(2):
            back = apply_left(txh[row], txl[row], get(row, col))
            part[row][col] = apply_right(back, syh[col], syl[col], True)
    rows = []
    for row in range(2):
        even, odd = part[row]
        rows.append((even + odd, even - odd))
    return [
        [rows[0][half] + rows[1][half] for half in range(2)],
        [rows[0][half] - rows[1][half] for half in range(2)],
    ]


def gain(shift, mu_row, mu_col):
    return 1.0 / (shift + diffusion * (mu_row + mu_col))


def first_kernel(strength, place, u, rate, first, mur, muc, sxh, sxl, syh, syl, mirx, miry, even, odd, even_up, odd_up, fold):
    rows, cols = u.shape
    hr, hc = rows // 2, cols // 2
    s = strength[0]
    shift = 1.0 + linear_part * s
    outs, ups = (even, odd), (even_up, odd_up)

    def folded(value):
        bottom = flip_rows(value[hr:], mirx[...])
        top = value[:hr]
        return top[:, :hc], flip_cols(top[:, hc:], miry[...]), bottom[:, :hc], flip_cols(bottom[:, hc:], miry[...])

    def fill(value):
        a, b, c, d = folded(value)
        fold[:hr, :hc], fold[:hr, hc:], fold[hr:, :hc], fold[hr:, hc:] = a, b, c, d

    def get(row, col):
        return fold[row * hr : (row + 1) * hr, col * hc : (col + 1) * hc]

    tables = (sxh, sxl, syh, syl)
    fill(react(u[...], rate[...], s) + jnp.where(place[0] == 0, 1.0, 0.0) * first[...])

    def write(row, col, modes):
        block = slice(row * hr, (row + 1) * hr)
        value = modes * gain(shift, mur[block, :], muc[:, col * hc : (col + 1) * hc])
        outs[col][block, :] = value
        ups[col][block, :] = value

    to_modes(get, tables, write)

    @pl.when(place[0] == place[1] - 1)
    def _():
        fill(u[...])

        def lower(row, col, modes):
            block = slice(row * hr, (row + 1) * hr)
            ups[col][block, :] = ups[col][block, :] - modes

        to_modes(get, tables, lower)


def middle_kernel(strength, place, ve, vo, rate, first, mur, muc, sxh, sxl, txh, txl, syh, syl, even, odd, even_up, odd_up, fold):
    hr, hc = ve.shape[0] // 2, ve.shape[1]
    s = strength[0]
    shift = 1.0 + linear_part * s
    modes_in, outs, ups = (ve, vo), (even, odd), (even_up, odd_up)
    quads = from_modes(lambda r, c: modes_in[c][r * hr : (r + 1) * hr, :], (txh, txl, syh, syl))
    for r in range(2):
        for c in range(2):
            spot = (slice(r * hr, (r + 1) * hr), slice(c * hc, (c + 1) * hc))
            fold[spot] = react(quads[r][c], rate[spot], s) + first[spot]

    def get(row, col):
        return fold[row * hr : (row + 1) * hr, col * hc : (col + 1) * hc]

    last = jnp.where(place[0] == place[1] - 1, 1.0, 0.0)

    def write(row, col, modes):
        block = slice(row * hr, (row + 1) * hr)
        value = modes * gain(shift, mur[block, :], muc[:, col * hc : (col + 1) * hc])
        outs[col][block, :] = value
        ups[col][block, :] = value - last * modes_in[col][block, :]

    to_modes(get, (sxh, sxl, syh, syl), write)


def last_kernel(ve, vo, txh, txl, syh, syl, mirx, miry, out):
    hr, hc = ve.shape[0] // 2, ve.shape[1]
    modes_in = (ve, vo)
    quads = from_modes(lambda r, c: modes_in[c][r * hr : (r + 1) * hr, :], (txh, txl, syh, syl))
    out[:hr, :hc] = quads[0][0]
    out[:hr, hc:] = flip_cols(quads[0][1], miry[...])
    out[hr:, :hc] = flip_rows(quads[1][0], mirx[...])
    out[hr:, hc:] = flip_rows(flip_cols(quads[1][1], miry[...]), mirx[...])


def fold_kernel(place, rate, first, mirx, miry, rate_out, first_out):
    hr, hc = rate.shape[0] // 2, rate.shape[1] // 2
    start = jnp.where(place[0] == 0, 1.0, 0.0)
    for value, out, scale in ((rate, rate_out, 1.0), (first, first_out, start)):
        out[:hr, :hc] = scale * value[:hr, :hc]
        out[:hr, hc:] = scale * flip_cols(value[:hr, hc:], miry[...])
        bottom = scale * flip_rows(value[hr:], mirx[...])
        out[hr:, :hc] = bottom[:, :hc]
        out[hr:, hc:] = flip_cols(bottom[:, hc:], miry[...])


def params():
    return pltpu.CompilerParams(vmem_limit_bytes=48 << 20)


def scan_steps(field, up, count, position, gains):
    levels = count.bit_length() - 1
    total = up
    row = jnp.int32(0)
    kept = []
    for level in range(levels):
        step = 1 << level
        pairs = [(source, source ^ step) for source in range(count)]
        half = total.shape[0] // 2
        bit = (position >> level) & 1
        send = lax.dynamic_slice_in_dim(total, (1 - bit) * half, half)
        keep = lax.dynamic_slice_in_dim(total, bit * half, half)
        got = lax.ppermute(send, "tm", pairs)
        row = row + bit * half
        low = jnp.where(bit == 0, keep, got)
        high = jnp.where(bit == 0, got, keep)
        factor = gains(row, half, step)
        total = high + factor * low
        kept.append((low, factor, bit, pairs))
    full_gain = gains(row, total.shape[0], count)
    carry = alpha_factor * total / (1.0 - alpha_factor * full_gain)
    for low, factor, bit, pairs in reversed(kept):
        later = low + factor * carry
        own = jnp.where(bit == 0, carry, later)
        send = jnp.where(bit == 0, later, carry)
        got = lax.ppermute(send, "tm", pairs)
        carry = jnp.concatenate([jnp.where(bit == 0, own, got), jnp.where(bit == 0, got, own)], axis=0)
    return field + gains(jnp.int32(0), field.shape[0], 1) * carry


def body(initial_value, guess, rate_field, strength):
    count = lax.axis_size("tm")
    position = lax.axis_index("tm")
    state = guess[0]
    rows, cols = state.shape
    hr, hc = rows // 2, cols // 2
    shift = 1.0 + linear_part * strength[0]
    place = jnp.stack([position, jnp.int32(count)])

    tx, ty = sine_halves(rows), sine_halves(cols)
    sxh, sxl = (jnp.asarray(t) for t in halves(tx))
    txh, txl = (jnp.asarray(t) for t in halves(tx.transpose(0, 2, 1)))
    syh, syl = (jnp.asarray(t) for t in halves(ty))
    mirx = jnp.asarray(reversal(math.gcd(hr, 256)))
    miry = jnp.asarray(reversal(math.gcd(hc, 256)))
    mu_row, mu_col = jnp.asarray(sine_eigen(rows)), jnp.asarray(sine_eigen(cols))
    mur, muc = mu_row[:, None], mu_col[None, :]

    chunk = jax.ShapeDtypeStruct((rows, hc), f32)
    scratch = [pltpu.VMEM((rows, cols), f32)]

    def gains_of(col):
        def gains(row, height, power):
            piece = lax.dynamic_slice_in_dim(mu_row, row, height)
            value = gain(shift, piece[:, None], mu_col[None, col * hc : (col + 1) * hc])
            while power > 1:
                value = value * value
                power //= 2
            return value

        return gains

    field_up = pl.pallas_call(
        first_kernel,
        out_shape=[chunk] * 4,
        in_specs=[SMEM] * 2 + [VMEM] * 11,
        out_specs=[VMEM] * 4,
        scratch_shapes=scratch,
        compiler_params=params(),
        name="first",
    )(strength, place, state, rate_field, initial_value, mur, muc, sxh, sxl, syh, syl, mirx, miry)
    rate_folded, first_folded = pl.pallas_call(
        fold_kernel,
        out_shape=[jax.ShapeDtypeStruct((rows, cols), f32)] * 2,
        in_specs=[SMEM] + [VMEM] * 4,
        out_specs=[VMEM] * 2,
        compiler_params=params(),
        name="fold",
    )(place, rate_field, initial_value, mirx, miry)
    for sweep_index in range(SWEEPS):
        modes = []
        for col in range(2):
            with jax.named_scope(f"scan_{sweep_index}_{col}"):
                modes.append(scan_steps(field_up[col], field_up[2 + col], count, position, gains_of(col)))
        if sweep_index < SWEEPS - 1:
            field_up = pl.pallas_call(
                middle_kernel,
                out_shape=[chunk] * 4,
                in_specs=[SMEM] * 2 + [VMEM] * 12,
                out_specs=[VMEM] * 4,
                scratch_shapes=scratch,
                compiler_params=params(),
                name="middle",
            )(strength, place, *modes, rate_folded, first_folded, mur, muc, sxh, sxl, txh, txl, syh, syl)
    result = pl.pallas_call(
        last_kernel,
        out_shape=jax.ShapeDtypeStruct((rows, cols), f32),
        in_specs=[VMEM] * 8,
        out_specs=VMEM,
        compiler_params=params(),
        name="last",
    )(*modes, txh, txl, syh, syl, mirx, miry)
    return result[None]


def solution(mesh):
    in_specs = (P("groups", None), P(("groups", "tm"), None, None), P(), P("groups"))
    out_specs = P(("groups", "tm"), None, None)
    return jax.shard_map(body, mesh=mesh, in_specs=in_specs, out_specs=out_specs, check_vma=False)
```

time: 453 us -> 214 us (0.47); the launches traced: 446 us -> 213 us
  blocking collectives: 165 us -> 0 us
  matrix products: 152 us -> 0 us
  starting transfers between devices: 14.1 us -> 76.3 us
  Pallas kernels: 0 us -> 26.9 us
  waiting for transfers between devices: 86.5 us -> 74.8 us
    all_to_all x3 -> x0, blocking collectives: 165 us -> none  [the longest x2 111 us: body(): lax.all_to_all(solved, 'tm', split_axis=0, concat_axis=1, tiled=True)]
    dot_general x16 -> x0, matrix products: 152 us -> none  [the longest x4 96.1 us: to_sine(): jnp.dot(jnp.dot(row_table, surface, precision=highest), col_table, precis...]
    ppermute x2 -> x32, starting transfers between devices: 7.02 us -> 76.3 us  [scan_steps(): got = lax.ppermute(send, 'tm', pairs)]
    all_to_all x1 -> x0, waiting for transfers between devices: 41.2 us -> none  [body(): lax.all_to_all((spectral * own_scale)[None], 'tm', split_axis=1, concat_a...]
    ppermute x2 -> x32, waiting for transfers between devices: 45.3 us -> 74.8 us  [scan_steps(): got = lax.ppermute(send, 'tm', pairs)]
    pallas_call x0 -> x4, Pallas kernels: none -> 26.9 us  [the longest x1 10.3 us: body(): pl.pallas_call(middle_kernel, out_shape=[chunk] * 4, in_specs=[SMEM] * 2...]
    all_to_all x2 -> x0, other arithmetic: 13.7 us -> none  [body(): lax.all_to_all((spectral * own_scale)[None], 'tm', split_axis=1, concat_a...]
    select_n x0 -> x43, other arithmetic: none -> 11.5 us  [the longest x15 5.47 us: scan_steps(): send = jnp.where(bit == 0, later, carry)]
  transfers between devices with their start and end apart: 3 -> 32, of which waited for: 3 -> 27; matrix products, arithmetic and copies ran while one was open for 0% -> 2% of each run, Pallas kernels for 0% -> 2%
where the time goes in v1:
time: 214 us; the launch traced here: 213 us
  starting transfers between devices  76.3 us (36%)
  waiting for transfers between devices  74.8 us (35%)
  Pallas kernels  26.9 us (13%)
  other arithmetic  17.7 us (8%)
  local copies, waits for them, and re-layouts  16.1 us (8%)
    ppermute x32, starting transfers between devices, scan_steps(): got = lax.ppermute(send, 'tm', pairs)  76.3 us
    ppermute x32, waiting for transfers between devices, scan_steps(): got = lax.ppermute(send, 'tm', pairs)  74.8 us
    unnamed x60, local copies, waits for them, and re-layouts  10.9 us
    pallas_call x1, Pallas kernels, body(): pl.pallas_call(middle_kernel, out_shape=[chunk] * 4, in_specs=[SMEM] * 2...  10.3 us
    pallas_call x1, Pallas kernels, body(): pl.pallas_call(first_kernel, out_shape=[chunk] * 4, in_specs=[SMEM] * 2 +...  7.63 us
    select_n x15, other arithmetic, scan_steps(): send = jnp.where(bit == 0, later, carry)  5.47 us
    select_n x16, other arithmetic, scan_steps(): jnp.where(bit == 0, own, got)  5.46 us
    pallas_call x1, Pallas kernels, body(): pl.pallas_call(last_kernel, out_shape=jax.ShapeDtypeStruct((rows, cols),...  5.21 us
  transfers between devices with their start and end apart: 32, of which 27 were waited for; matrix products, arithmetic and copies ran while one was open for 2% of the time, Pallas kernels for 2%

profile of v1, /device:TPU:1, one launch (start us, length us, event | category | flops | bytes accessed | tf_op | source)
XLA Modules:
  0.0 213.0 jit_solution(11584242893135128729)
XLA Ops:
  6.4 7.6 %first.3 = (f32[512,512]{1,0:T(8,128)S(1)}, f32[512,512]{1,0:T(8,128)S(1)}, f32[512,512]{1,0:T(8,128)S(1)}, f32[512,512]{1,0:T(8,128)S(1)}) custom-call(f32[1]{0:T(128)S(6)} %copy.15.strength, s32[2]{0:T(128)S(1)} %pad_add_fusion.place, f32[512,1024]{1,0:T(8,128)} %bitcast.4, f32[512,1024]{1,0:T(8,128)} %rate.3, f32[512,1024]{1,0:T(8,128)} %first.5, ...), custom_call_target="tpu_custom_call" | custom-call | tf_op jit(solution)/shard_map/first/pallas_call | solution.py:282
  20.2 2.4 %collective-permute-start.9 = (f32[128,512]{1,0:T(8,128)S(1)}, f32[128,512]{1,0:T(8,128)}, u32[]{:S(2)}, u32[]{:S(2)}) collective-permute-start(f32[128,512]{1,0:T(8,128)S(1)} %constant_dynamic-slice_fusion.10), channel_id=1, source_target_pairs={{0,2},{1,3},{2,0},{3,1},{4,6},{5,7},{6,4},{7,5},{8,10},{9,11},{10,... | collective-permute-start | bytes 786440 | tf_op jit(solution)/shard_map/scan_0_1/ppermute | solution.py:232
  22.7 6.3 %collective-permute-done.9 = f32[128,512]{1,0:T(8,128)} collective-permute-done((f32[128,512]{1,0:T(8,128)S(1)}, f32[128,512]{1,0:T(8,128)}, u32[]{:S(2)}, u32[]{:S(2)}) %collective-permute-start.9) | collective-permute-done | bytes 262176 | tf_op jit(solution)/shard_map/scan_0_1/ppermute | solution.py:232
  36.8 6.8 %collective-permute-start.11 = (f32[32,512]{1,0:T(8,128)}, f32[32,512]{1,0:T(8,128)}, u32[]{:S(2)}, u32[]{:S(2)}) collective-permute-start(f32[32,512]{1,0:T(8,128)} %constant_dynamic-slice_fusion.8), channel_id=1, source_target_pairs={{0,8},{1,9},{2,10},{3,11},{4,12},{5,13},{6,14},{7,15},{8,0},{9,1},... | collective-permute-start | bytes 196616 | tf_op jit(solution)/shard_map/scan_0_1/ppermute | solution.py:232
  46.6 2.5 %collective-permute-start.12 = (f32[32,512]{1,0:T(8,128)S(1)}, f32[32,512]{1,0:T(8,128)S(1)}, u32[]{:S(2)}, u32[]{:S(2)}) collective-permute-start(f32[32,512]{1,0:T(8,128)S(1)} %fusion.32), channel_id=1, source_target_pairs={{0,8},{1,9},{2,10},{3,11},{4,12},{5,13},{6,14},{7,15},{8,0},{9,1},... | collective-permute-start | bytes 196616 | tf_op jit(solution)/shard_map/scan_0_1/ppermute | solution.py:245
  59.3 5.0 %collective-permute-start = (f32[256,512]{1,0:T(8,128)S(1)}, f32[256,512]{1,0:T(8,128)S(1)}, u32[]{:S(2)}, u32[]{:S(2)}) collective-permute-start(f32[256,512]{1,0:T(8,128)S(1)} %constant_dynamic-slice_fusion.15), channel_id=1, source_target_pairs={{0,1},{1,0},{2,3},{3,2},{4,5},{5,4},{6,7},{7,6},{8,9},{9,8},{10,11... | collective-permute-start | bytes 1572872 | tf_op jit(solution)/shard_map/scan_0_0/ppermute | solution.py:232
  67.4 5.2 %collective-permute-done.1 = f32[128,512]{1,0:T(8,128)S(1)} collective-permute-done((f32[128,512]{1,0:T(8,128)S(1)}, f32[128,512]{1,0:T(8,128)S(1)}, u32[]{:S(2)}, u32[]{:S(2)}) %collective-permute-start.1) | collective-permute-done | bytes 262176 | tf_op jit(solution)/shard_map/scan_0_0/ppermute | solution.py:232
  77.0 2.7 %collective-permute-start.3 = (f32[32,512]{1,0:T(8,128)S(1)}, f32[32,512]{1,0:T(8,128)S(1)}, u32[]{:S(2)}, u32[]{:S(2)}) collective-permute-start(f32[32,512]{1,0:T(8,128)S(1)} %constant_dynamic-slice_fusion.12), channel_id=1, source_target_pairs={{0,8},{1,9},{2,10},{3,11},{4,12},{5,13},{6,14},{7,15},{8,0},{9,1},... | collective-permute-start | bytes 196616 | tf_op jit(solution)/shard_map/scan_0_0/ppermute | solution.py:232
  81.8 2.9 %collective-permute-start.4 = (f32[32,512]{1,0:T(8,128)S(1)}, f32[32,512]{1,0:T(8,128)S(1)}, u32[]{:S(2)}, u32[]{:S(2)}) collective-permute-start(f32[32,512]{1,0:T(8,128)S(1)} %fusion.30), channel_id=1, source_target_pairs={{0,8},{1,9},{2,10},{3,11},{4,12},{5,13},{6,14},{7,15},{8,0},{9,1},... | collective-permute-start | bytes 196616 | tf_op jit(solution)/shard_map/scan_0_0/ppermute | solution.py:245
  86.6 2.7 %collective-permute-start.5 = (f32[64,512]{1,0:T(8,128)S(1)}, f32[64,512]{1,0:T(8,128)S(1)}, u32[]{:S(2)}, u32[]{:S(2)}) collective-permute-start(f32[64,512]{1,0:T(8,128)S(1)} %fusion.26), channel_id=1, source_target_pairs={{0,4},{1,5},{2,6},{3,7},{4,0},{5,1},{6,2},{7,3},{8,12},{9,13},{10,... | collective-permute-start | bytes 393224 | tf_op jit(solution)/shard_map/scan_0_0/ppermute | solution.py:245
  92.0 8.5 %collective-permute-start.15 = (f32[256,512]{1,0:T(8,128)S(1)}, f32[256,512]{1,0:T(8,128)S(1)}, u32[]{:S(2)}, u32[]{:S(2)}) collective-permute-start(f32[256,512]{1,0:T(8,128)S(1)} %get-tuple-element.63), channel_id=1, source_target_pairs={{0,1},{1,0},{2,3},{3,2},{4,5},{5,4},{6,7},{7,6},{8,9},{9,8},{10,11... | collective-permute-start | bytes 1572872 | tf_op jit(solution)/shard_map/scan_0_1/ppermute | solution.py:245
  103.5 3.6 %collective-permute-start.7 = (f32[256,512]{1,0:T(8,128)S(1)}, f32[256,512]{1,0:T(8,128)S(1)}, u32[]{:S(2)}, u32[]{:S(2)}) collective-permute-start(f32[256,512]{1,0:T(8,128)S(1)} %get-tuple-element.62), channel_id=1, source_target_pairs={{0,1},{1,0},{2,3},{3,2},{4,5},{5,4},{6,7},{7,6},{8,9},{9,8},{10,11... | collective-permute-start | bytes 1572872 | tf_op jit(solution)/shard_map/scan_0_0/ppermute | solution.py:245
  107.1 3.7 %fold.1 = (f32[512,1024]{1,0:T(8,128)S(1)}, f32[512,1024]{1,0:T(8,128)S(1)}) custom-call(s32[2]{0:T(128)S(1)} %pad_add_fusion.place, f32[512,1024]{1,0:T(8,128)} %rate.3, f32[512,1024]{1,0:T(8,128)} %first.5, bf16[256,256]{1,0:T(8,128)(2,1)S(1)} %copy-done.4, bf16[256,256]{1,0:T(8,128)(2,1)S(1)} %copy-done.4), custom_call_target="tpu_custom_call" | custom-call | tf_op jit(solution)/shard_map/fold/pallas_call | solution.py:291
  114.9 10.3 %middle.1 = (f32[512,512]{1,0:T(8,128)S(1)}, f32[512,512]{1,0:T(8,128)S(1)}, f32[512,512]{1,0:T(8,128)S(1)}, f32[512,512]{1,0:T(8,128)S(1)}) custom-call(f32[1]{0:T(128)S(6)} %copy.15.strength, s32[2]{0:T(128)S(1)} %pad_add_fusion.place, f32[512,512]{1,0:T(8,128)} %get-tuple-element.60.ve, f32[512,512]{1,0:T(8,128)} %get-tuple-element.59.vo, ...), custom_call_target="tpu_custom_call" | custom-call | tf_op jit(solution)/shard_map/middle/pallas_call | solution.py:305
  127.8 7.3 %collective-permute-done.25 = f32[128,512]{1,0:T(8,128)S(1)} collective-permute-done((f32[128,512]{1,0:T(8,128)S(1)}, f32[128,512]{1,0:T(8,128)S(1)}, u32[]{:S(2)}, u32[]{:S(2)}) %collective-permute-start.25) | collective-permute-done | bytes 262176 | tf_op jit(solution)/shard_map/scan_1_1/ppermute | solution.py:232
  145.7 2.6 %collective-permute-done.28 = f32[32,512]{1,0:T(8,128)S(1)} collective-permute-done((f32[32,512]{1,0:T(8,128)S(1)}, f32[32,512]{1,0:T(8,128)S(1)}, u32[]{:S(2)}, u32[]{:S(2)}) %collective-permute-start.28) | collective-permute-done | bytes 65568 | tf_op jit(solution)/shard_map/scan_1_1/ppermute | solution.py:245
  149.8 3.1 %collective-permute-done.29 = f32[64,512]{1,0:T(8,128)S(1)} collective-permute-done((f32[64,512]{1,0:T(8,128)S(1)}, f32[64,512]{1,0:T(8,128)S(1)}, u32[]{:S(2)}, u32[]{:S(2)}) %collective-permute-start.29) | collective-permute-done | bytes 131104 | tf_op jit(solution)/shard_map/scan_1_1/ppermute | solution.py:245
  153.5 5.1 %collective-permute-start.16 = (f32[256,512]{1,0:T(8,128)S(1)}, f32[256,512]{1,0:T(8,128)S(1)}, u32[]{:S(2)}, u32[]{:S(2)}) collective-permute-start(f32[256,512]{1,0:T(8,128)S(1)} %constant_dynamic-slice_fusion.7), channel_id=1, source_target_pairs={{0,1},{1,0},{2,3},{3,2},{4,5},{5,4},{6,7},{7,6},{8,9},{9,8},{10,11... | collective-permute-start | bytes 1572872 | tf_op jit(solution)/shard_map/scan_1_0/ppermute | solution.py:232
  159.0 6.0 %collective-permute-start.31 = (f32[256,512]{1,0:T(8,128)S(1)}, f32[256,512]{1,0:T(8,128)S(1)}, u32[]{:S(2)}, u32[]{:S(2)}) collective-permute-start(f32[256,512]{1,0:T(8,128)S(1)} %fusion.4), channel_id=1, source_target_pairs={{0,1},{1,0},{2,3},{3,2},{4,5},{5,4},{6,7},{7,6},{8,9},{9,8},{10,11... | collective-permute-start | bytes 1572872 | tf_op jit(solution)/shard_map/scan_1_1/ppermute | solution.py:245
  167.1 7.5 %collective-permute-done.17 = f32[128,512]{1,0:T(8,128)S(1)} collective-permute-done((f32[128,512]{1,0:T(8,128)S(1)}, f32[128,512]{1,0:T(8,128)S(1)}, u32[]{:S(2)}, u32[]{:S(2)}) %collective-permute-start.17) | collective-permute-done | bytes 262176 | tf_op jit(solution)/shard_map/scan_1_0/ppermute | solution.py:232
  189.3 3.1 %collective-permute-done.21 = f32[64,512]{1,0:T(8,128)S(1)} collective-permute-done((f32[64,512]{1,0:T(8,128)S(1)}, f32[64,512]{1,0:T(8,128)S(1)}, u32[]{:S(2)}, u32[]{:S(2)}) %collective-permute-start.21) | collective-permute-done | bytes 131104 | tf_op jit(solution)/shard_map/scan_1_0/ppermute | solution.py:245
  193.1 4.9 %collective-permute-done.22 = f32[128,512]{1,0:T(8,128)S(1)} collective-permute-done((f32[128,512]{1,0:T(8,128)S(1)}, f32[128,512]{1,0:T(8,128)S(1)}, u32[]{:S(2)}, u32[]{:S(2)}) %collective-permute-start.22) | collective-permute-done | bytes 262176 | tf_op jit(solution)/shard_map/scan_1_0/ppermute | solution.py:245
  198.4 6.0 %collective-permute-start.23 = (f32[256,512]{1,0:T(8,128)S(1)}, f32[256,512]{1,0:T(8,128)S(1)}, u32[]{:S(2)}, u32[]{:S(2)}) collective-permute-start(f32[256,512]{1,0:T(8,128)S(1)} %fusion.6), channel_id=1, source_target_pairs={{0,1},{1,0},{2,3},{3,2},{4,5},{5,4},{6,7},{7,6},{8,9},{9,8},{10,11... | collective-permute-start | bytes 1572872 | tf_op jit(solution)/shard_map/scan_1_0/ppermute | solution.py:245
  207.8 5.2 %last.1 = f32[512,1024]{1,0:T(8,128)} custom-call(f32[512,512]{1,0:T(8,128)S(1)} %get-tuple-element.58.ve, f32[512,512]{1,0:T(8,128)S(1)} %get-tuple-element.57.vo, bf16[2,256,256]{2,1,0:T(8,128)(2,1)S(1)} %copy-done.8, bf16[2,256,256]{2,1,0:T(8,128)(2,1)S(1)} %copy-done.7, bf16[2,512,512]{2,1,0:T(8,128)(2,1)S(1)} %copy-done.2, ...), custom_call_target="tpu_custom_call" | custom-call | tf_op jit(solution)/shard_map/last/pallas_call | solution.py:314
  (180 shorter events, 90.6 us)
Async XLA Ops:
  20.2 8.9 %collective-permute-start.9 = (f32[128,512]{1,0:T(8,128)S(1)}, f32[128,512]{1,0:T(8,128)}, u32[]{:S(2)}, u32[]{:S(2)}) collective-permute-start(f32[128,512]{1,0:T(8,128)S(1)} %constant_dynamic-slice_fusion.10), channel_id=1, source_target_pairs={{0,2},{1,3},{2,0},{3,1},{4,6},{5,7},{6,4},{7,5},{8,10},{9,11},{10,... | collective-permute-start | bytes 786440 | tf_op jit(solution)/shard_map/scan_0_1/ppermute | solution.py:232
  36.8 8.7 %collective-permute-start.11 = (f32[32,512]{1,0:T(8,128)}, f32[32,512]{1,0:T(8,128)}, u32[]{:S(2)}, u32[]{:S(2)}) collective-permute-start(f32[32,512]{1,0:T(8,128)} %constant_dynamic-slice_fusion.8), channel_id=1, source_target_pairs={{0,8},{1,9},{2,10},{3,11},{4,12},{5,13},{6,14},{7,15},{8,0},{9,1},... | collective-permute-start | bytes 196616 | tf_op jit(solution)/shard_map/scan_0_1/ppermute | solution.py:232
  52.4 4.2 %collective-permute-start.13 = (f32[64,512]{1,0:T(8,128)S(1)}, f32[64,512]{1,0:T(8,128)S(1)}, u32[]{:S(2)}, u32[]{:S(2)}) collective-permute-start(f32[64,512]{1,0:T(8,128)S(1)} %fusion.24), channel_id=1, source_target_pairs={{0,4},{1,5},{2,6},{3,7},{4,0},{5,1},{6,2},{7,3},{8,12},{9,13},{10,... | collective-permute-start | bytes 393224 | tf_op jit(solution)/shard_map/scan_0_1/ppermute | solution.py:245
  58.3 6.0 %collective-permute-start.14 = (f32[128,512]{1,0:T(8,128)S(1)}, f32[128,512]{1,0:T(8,128)S(1)}, u32[]{:S(2)}, u32[]{:S(2)}) collective-permute-start(f32[128,512]{1,0:T(8,128)S(1)} %fusion.16), channel_id=1, source_target_pairs={{0,2},{1,3},{2,0},{3,1},{4,6},{5,7},{6,4},{7,5},{8,10},{9,11},{10,... | collective-permute-start | bytes 786440 | tf_op jit(solution)/shard_map/scan_0_1/ppermute | solution.py:245
  59.3 6.6 %collective-permute-start = (f32[256,512]{1,0:T(8,128)S(1)}, f32[256,512]{1,0:T(8,128)S(1)}, u32[]{:S(2)}, u32[]{:S(2)}) collective-permute-start(f32[256,512]{1,0:T(8,128)S(1)} %constant_dynamic-slice_fusion.15), channel_id=1, source_target_pairs={{0,1},{1,0},{2,3},{3,2},{4,5},{5,4},{6,7},{7,6},{8,9},{9,8},{10,11... | collective-permute-start | bytes 1572872 | tf_op jit(solution)/shard_map/scan_0_0/ppermute | solution.py:232
  67.3 5.3 %collective-permute-start.1 = (f32[128,512]{1,0:T(8,128)S(1)}, f32[128,512]{1,0:T(8,128)S(1)}, u32[]{:S(2)}, u32[]{:S(2)}) collective-permute-start(f32[128,512]{1,0:T(8,128)S(1)} %constant_dynamic-slice_fusion.14), channel_id=1, source_target_pairs={{0,2},{1,3},{2,0},{3,1},{4,6},{5,7},{6,4},{7,5},{8,10},{9,11},{10,... | collective-permute-start | bytes 786440 | tf_op jit(solution)/shard_map/scan_0_0/ppermute | solution.py:232
  72.8 4.2 %collective-permute-start.2 = (f32[64,512]{1,0:T(8,128)S(1)}, f32[64,512]{1,0:T(8,128)S(1)}, u32[]{:S(2)}, u32[]{:S(2)}) collective-permute-start(f32[64,512]{1,0:T(8,128)S(1)} %constant_dynamic-slice_fusion.13), channel_id=1, source_target_pairs={{0,4},{1,5},{2,6},{3,7},{4,0},{5,1},{6,2},{7,3},{8,12},{9,13},{10,... | collective-permute-start | bytes 393224 | tf_op jit(solution)/shard_map/scan_0_0/ppermute | solution.py:232
  77.0 4.7 %collective-permute-start.3 = (f32[32,512]{1,0:T(8,128)S(1)}, f32[32,512]{1,0:T(8,128)S(1)}, u32[]{:S(2)}, u32[]{:S(2)}) collective-permute-start(f32[32,512]{1,0:T(8,128)S(1)} %constant_dynamic-slice_fusion.12), channel_id=1, source_target_pairs={{0,8},{1,9},{2,10},{3,11},{4,12},{5,13},{6,14},{7,15},{8,0},{9,1},... | collective-permute-start | bytes 196616 | tf_op jit(solution)/shard_map/scan_0_0/ppermute | solution.py:232
  81.8 4.6 %collective-permute-start.4 = (f32[32,512]{1,0:T(8,128)S(1)}, f32[32,512]{1,0:T(8,128)S(1)}, u32[]{:S(2)}, u32[]{:S(2)}) collective-permute-start(f32[32,512]{1,0:T(8,128)S(1)} %fusion.30), channel_id=1, source_target_pairs={{0,8},{1,9},{2,10},{3,11},{4,12},{5,13},{6,14},{7,15},{8,0},{9,1},... | collective-permute-start | bytes 196616 | tf_op jit(solution)/shard_map/scan_0_0/ppermute | solution.py:245
  86.6 5.0 %collective-permute-start.5 = (f32[64,512]{1,0:T(8,128)S(1)}, f32[64,512]{1,0:T(8,128)S(1)}, u32[]{:S(2)}, u32[]{:S(2)}) collective-permute-start(f32[64,512]{1,0:T(8,128)S(1)} %fusion.26), channel_id=1, source_target_pairs={{0,4},{1,5},{2,6},{3,7},{4,0},{5,1},{6,2},{7,3},{8,12},{9,13},{10,... | collective-permute-start | bytes 393224 | tf_op jit(solution)/shard_map/scan_0_0/ppermute | solution.py:245
  91.9 8.6 %collective-permute-start.6 = (f32[128,512]{1,0:T(8,128)S(1)}, f32[128,512]{1,0:T(8,128)S(1)}, u32[]{:S(2)}, u32[]{:S(2)}) collective-permute-start(f32[128,512]{1,0:T(8,128)S(1)} %fusion.18), channel_id=1, source_target_pairs={{0,2},{1,3},{2,0},{3,1},{4,6},{5,7},{6,4},{7,5},{8,10},{9,11},{10,... | collective-permute-start | bytes 786440 | tf_op jit(solution)/shard_map/scan_0_0/ppermute | solution.py:245
  92.0 10.0 %collective-permute-start.15 = (f32[256,512]{1,0:T(8,128)S(1)}, f32[256,512]{1,0:T(8,128)S(1)}, u32[]{:S(2)}, u32[]{:S(2)}) collective-permute-start(f32[256,512]{1,0:T(8,128)S(1)} %get-tuple-element.63), channel_id=1, source_target_pairs={{0,1},{1,0},{2,3},{3,2},{4,5},{5,4},{6,7},{7,6},{8,9},{9,8},{10,11... | collective-permute-start | bytes 1572872 | tf_op jit(solution)/shard_map/scan_0_1/ppermute | solution.py:245
  103.5 7.5 %collective-permute-start.7 = (f32[256,512]{1,0:T(8,128)S(1)}, f32[256,512]{1,0:T(8,128)S(1)}, u32[]{:S(2)}, u32[]{:S(2)}) collective-permute-start(f32[256,512]{1,0:T(8,128)S(1)} %get-tuple-element.62), channel_id=1, source_target_pairs={{0,1},{1,0},{2,3},{3,2},{4,5},{5,4},{6,7},{7,6},{8,9},{9,8},{10,11... | collective-permute-start | bytes 1572872 | tf_op jit(solution)/shard_map/scan_0_0/ppermute | solution.py:245
  127.5 7.6 %collective-permute-start.25 = (f32[128,512]{1,0:T(8,128)S(1)}, f32[128,512]{1,0:T(8,128)S(1)}, u32[]{:S(2)}, u32[]{:S(2)}) collective-permute-start(f32[128,512]{1,0:T(8,128)S(1)} %constant_dynamic-slice_fusion.2), channel_id=1, source_target_pairs={{0,2},{1,3},{2,0},{3,1},{4,6},{5,7},{6,4},{7,5},{8,10},{9,11},{10,... | collective-permute-start | bytes 786440 | tf_op jit(solution)/shard_map/scan_1_1/ppermute | solution.py:232
  143.7 4.6 %collective-permute-start.28 = (f32[32,512]{1,0:T(8,128)S(1)}, f32[32,512]{1,0:T(8,128)S(1)}, u32[]{:S(2)}, u32[]{:S(2)}) collective-permute-start(f32[32,512]{1,0:T(8,128)S(1)} %fusion.36), channel_id=1, source_target_pairs={{0,8},{1,9},{2,10},{3,11},{4,12},{5,13},{6,14},{7,15},{8,0},{9,1},... | collective-permute-start | bytes 196616 | tf_op jit(solution)/shard_map/scan_1_1/ppermute | solution.py:245
  153.2 5.4 %collective-permute-start.30 = (f32[128,512]{1,0:T(8,128)S(1)}, f32[128,512]{1,0:T(8,128)S(1)}, u32[]{:S(2)}, u32[]{:S(2)}) collective-permute-start(f32[128,512]{1,0:T(8,128)S(1)} %fusion.12), channel_id=1, source_target_pairs={{0,2},{1,3},{2,0},{3,1},{4,6},{5,7},{6,4},{7,5},{8,10},{9,11},{10,... | collective-permute-start | bytes 786440 | tf_op jit(solution)/shard_map/scan_1_1/ppermute | solution.py:245
  153.5 11.6 %collective-permute-start.16 = (f32[256,512]{1,0:T(8,128)S(1)}, f32[256,512]{1,0:T(8,128)S(1)}, u32[]{:S(2)}, u32[]{:S(2)}) collective-permute-start(f32[256,512]{1,0:T(8,128)S(1)} %constant_dynamic-slice_fusion.7), channel_id=1, source_target_pairs={{0,1},{1,0},{2,3},{3,2},{4,5},{5,4},{6,7},{7,6},{8,9},{9,8},{10,11... | collective-permute-start | bytes 1572872 | tf_op jit(solution)/shard_map/scan_1_0/ppermute | solution.py:232
  159.0 7.6 %collective-permute-start.31 = (f32[256,512]{1,0:T(8,128)S(1)}, f32[256,512]{1,0:T(8,128)S(1)}, u32[]{:S(2)}, u32[]{:S(2)}) collective-permute-start(f32[256,512]{1,0:T(8,128)S(1)} %fusion.4), channel_id=1, source_target_pairs={{0,1},{1,0},{2,3},{3,2},{4,5},{5,4},{6,7},{7,6},{8,9},{9,8},{10,11... | collective-permute-start | bytes 1572872 | tf_op jit(solution)/shard_map/scan_1_1/ppermute | solution.py:245
  167.0 7.6 %collective-permute-start.17 = (f32[128,512]{1,0:T(8,128)S(1)}, f32[128,512]{1,0:T(8,128)S(1)}, u32[]{:S(2)}, u32[]{:S(2)}) collective-permute-start(f32[128,512]{1,0:T(8,128)S(1)} %constant_dynamic-slice_fusion.6), channel_id=1, source_target_pairs={{0,2},{1,3},{2,0},{3,1},{4,6},{5,7},{6,4},{7,5},{8,10},{9,11},{10,... | collective-permute-start | bytes 786440 | tf_op jit(solution)/shard_map/scan_1_0/ppermute | solution.py:232
  174.7 4.2 %collective-permute-start.18 = (f32[64,512]{1,0:T(8,128)S(1)}, f32[64,512]{1,0:T(8,128)S(1)}, u32[]{:S(2)}, u32[]{:S(2)}) collective-permute-start(f32[64,512]{1,0:T(8,128)S(1)} %constant_dynamic-slice_fusion.5), channel_id=1, source_target_pairs={{0,4},{1,5},{2,6},{3,7},{4,0},{5,1},{6,2},{7,3},{8,12},{9,13},{10,... | collective-permute-start | bytes 393224 | tf_op jit(solution)/shard_map/scan_1_0/ppermute | solution.py:232
  183.2 4.6 %collective-permute-start.20 = (f32[32,512]{1,0:T(8,128)S(1)}, f32[32,512]{1,0:T(8,128)S(1)}, u32[]{:S(2)}, u32[]{:S(2)}) collective-permute-start(f32[32,512]{1,0:T(8,128)S(1)} %fusion.34), channel_id=1, source_target_pairs={{0,8},{1,9},{2,10},{3,11},{4,12},{5,13},{6,14},{7,15},{8,0},{9,1},... | collective-permute-start | bytes 196616 | tf_op jit(solution)/shard_map/scan_1_0/ppermute | solution.py:245
  188.0 4.4 %collective-permute-start.21 = (f32[64,512]{1,0:T(8,128)S(1)}, f32[64,512]{1,0:T(8,128)S(1)}, u32[]{:S(2)}, u32[]{:S(2)}) collective-permute-start(f32[64,512]{1,0:T(8,128)S(1)} %fusion.22), channel_id=1, source_target_pairs={{0,4},{1,5},{2,6},{3,7},{4,0},{5,1},{6,2},{7,3},{8,12},{9,13},{10,... | collective-permute-start | bytes 393224 | tf_op jit(solution)/shard_map/scan_1_0/ppermute | solution.py:245
  192.7 5.3 %collective-permute-start.22 = (f32[128,512]{1,0:T(8,128)S(1)}, f32[128,512]{1,0:T(8,128)S(1)}, u32[]{:S(2)}, u32[]{:S(2)}) collective-permute-start(f32[128,512]{1,0:T(8,128)S(1)} %fusion.14), channel_id=1, source_target_pairs={{0,2},{1,3},{2,0},{3,1},{4,6},{5,7},{6,4},{7,5},{8,10},{9,11},{10,... | collective-permute-start | bytes 786440 | tf_op jit(solution)/shard_map/scan_1_0/ppermute | solution.py:245
  198.4 7.5 %collective-permute-start.23 = (f32[256,512]{1,0:T(8,128)S(1)}, f32[256,512]{1,0:T(8,128)S(1)}, u32[]{:S(2)}, u32[]{:S(2)}) collective-permute-start(f32[256,512]{1,0:T(8,128)S(1)} %fusion.6), channel_id=1, source_target_pairs={{0,1},{1,0},{2,3},{3,2},{4,5},{5,4},{6,7},{7,6},{8,9},{9,8},{10,11... | collective-permute-start | bytes 1572872 | tf_op jit(solution)/shard_map/scan_1_0/ppermute | solution.py:245
  (38 other events, 173.8 us)
